TPU v7x, 256 devices: a whole 4x4x8 slice. The times are simulated.
256 devices in a mesh: modes: 64 (over y, x, z_hi), mom: 4 (over z_lo, core).
Axes of the slice: x: 4, y: 4, z: 8 (z_hi: 4, z_lo: 2; z = z_hi * 2 + z_lo), core: 2. Of those that a mesh axis runs over, the one named last changes fastest.
Arguments:
- elementals: float32 [2, 8, 256, 256, 256], P(None, 'mom', 'modes'), parts along dimension 1, may hold values from -64 to 64
- perambulators: float32 [64, 2, 2, 256, 256], P('modes'), may hold values from -0.25 to 0.25
- owners: int32 [2], replicated, may hold values from 0 to 63
- pairing: int32 [8], P('mom'), parts along dimension 0, may hold values from 0 to 1
Outputs:
- propagated: bfloat16 [2, 8, 2, 256, 256, 256], P(None, 'mom', None, 'modes'), parts along dimension 1
- correlator: float32 [2, 8, 2], P(None, 'mom'), parts along dimension 1
There are 4 independent parts, one for each index of `mom`. A program takes and returns all parts, laid end to end along the dimension named above; an argument that names none is the same for every part. Nothing has to cross between parts.
All inputs are finite; a program needn't handle non-finite values.
Results may differ from a plain program's by a relative error of at most 0.001.
Values sent between devices are 32-bit elements; how exact they have to be, the bound alone decides.
No kernel may reach another device: no remote copies, remote signals or barrier semaphores. Data moves between devices by JAX's collectives and lax.ppermute only.
A program may use at most 128 MiB of HBM per device.

v0:
```python
import jax
import jax.numpy as jnp
from jax import lax
from jax.sharding import PartitionSpec as P

N = 256
highest = lax.Precision.HIGHEST


def spread(block, axis, source):
    block = jnp.where(lax.axis_index(axis) == source, block, jnp.zeros_like(block))
    return lax.psum(block, axis)


def complex_product(formula, matrix_re, matrix_im, tensor_re, tensor_im):

    def single(left_part, right_part):
        return jnp.einsum(formula, left_part, right_part, precision=highest)

    real_part = single(matrix_re, tensor_re) - single(matrix_im, tensor_im)
    imag_part = single(matrix_re, tensor_im) + single(matrix_im, tensor_re)
    return (real_part, imag_part)


def local_pair(elem_re, elem_im, peram_re, peram_im):
    third_re, third_im = complex_product("kc,abc->abk", peram_re, peram_im, elem_re, elem_im)
    result = complex_product("jb,abk->kaj", peram_re, peram_im, third_re, third_im)
    return result


def shards(elementals, perambulators, owners, pairing):
    mom_count = elementals.shape[1]
    time_count = perambulators.shape[1]
    norm_scale = float(N) ** (-1.5)
    perams = []
    for time_index in range(time_count):
        perams.append(spread(perambulators[0, time_index], "modes", owners[time_index]))
    sink_slabs = []
    for mom_index in range(mom_count):
        picked = lax.dynamic_index_in_dim(elementals, pairing[mom_index], 1, keepdims=False)
        sink_slabs.append((jnp.swapaxes(picked[0], 1, 2), jnp.swapaxes(picked[1], 1, 2)))
    carried_re = [[None] * time_count for mom_index in range(mom_count)]
    carried_im = [[None] * time_count for mom_index in range(mom_count)]
    sums_real = [[None] * time_count for mom_index in range(mom_count)]
    sums_imag = [[None] * time_count for mom_index in range(mom_count)]
    for time_index in range(time_count):
        peram_re = perams[time_index][0]
        peram_im = perams[time_index][1]
        outputs = []
        for mom_index in range(mom_count):
            slab_re, slab_im = local_pair(
                elementals[0, mom_index], elementals[1, mom_index], peram_re, peram_im
            )
            outputs.append(
                complex_product(
                    "ia,kaj->kij",
                    peram_re,
                    peram_im,
                    lax.all_to_all(slab_re, "modes", split_axis=0, concat_axis=1, tiled=True),
                    lax.all_to_all(slab_im, "modes", split_axis=0, concat_axis=1, tiled=True),
                )
            )
        for mom_index in range(mom_count):
            out_re, out_im = outputs[mom_index]
            sink_re, sink_im = sink_slabs[mom_index]
            sums_real[mom_index][time_index] = jnp.sum(sink_re * out_re + sink_im * out_im)
            sums_imag[mom_index][time_index] = jnp.sum(sink_re * out_im - sink_im * out_re)
            carried_re[mom_index][time_index] = out_re
            carried_im[mom_index][time_index] = out_im
    partial_sums = jnp.stack(
        [
            jnp.stack([jnp.stack(row) for row in sums_real]),
            jnp.stack([jnp.stack(row) for row in sums_imag]),
        ]
    )
    correlator = lax.psum(partial_sums, "modes") * norm_scale
    propagated = jnp.stack(
        [
            jnp.stack([jnp.stack(row) for row in carried_re]),
            jnp.stack([jnp.stack(row) for row in carried_im]),
        ]
    ).astype(jnp.bfloat16)
    return (propagated, correlator)


def solution(mesh):
    placed = (
        P(None, "mom", "modes", None, None),
        P("modes", None, None, None, None),
        P(),
        P("mom"),
    )
    return jax.shard_map(
        shards,
        mesh=mesh,
        in_specs=placed,
        out_specs=(P(None, "mom", None, "modes", None, None), P(None, "mom", None)),
        check_vma=False,
    )
```

profile of v0, /device:TPU:32, one launch (start us, length us, event | category | flops | bytes accessed | tf_op | source)
XLA Modules:
  0.0 1279.1 jit_solution(18263410880325923134)
XLA Ops:
  9.8 2.3 select_bitcast_fusion.1
  12.1 742.1 %all-reduce.3.cloned.1.call-done = (f32[2,256,256]{2,1,0:T(8,128)}, f32[2,256,256]{2,1,0:T(8,128)}) async-done(((f32[2,256,256]{2,1,0:T(8,128)}, f32[2,256,256]{2,1,0:T(8,128)}), (f32[2,256,256]{2,1,0:T(8,128)}, f32[2,256,256]{2,1,0:T(8,128)})) %all-reduce.3.cloned.1.call-update) | async-done | bytes 1048592 | tf_op jit(solution)/shard_map/psum | solution.py:12
  754.2 2.5 fusion.23
  756.7 2.4 fusion.16
  763.3 1.6 copy.58
  764.9 9.8 all-to-all-start.6
  776.8 1.6 copy.61
  778.4 27.7 %all-to-all-done.6 = f32[256,4,256]{2,1,0:T(4,128)} async-done(((f32[256,4,256]{2,1,0:T(4,128)}), f32[256,4,256]{2,1,0:T(4,128)}, u32[]{:S(2)}, u32[]{:S(2)}) %all-to-all-start.6) | async-done | bytes 1048608 | tf_op jit(solution)/shard_map/all_to_all | solution.py:59
  806.1 6.7 all-to-all-start.7
  812.8 2.4 fusion.28
  815.3 2.3 fusion.35
  821.7 1.7 copy.49
  823.4 18.2 %all-to-all-done.7 = f32[256,4,256]{2,1,0:T(4,128)} async-done(((f32[256,4,256]{2,1,0:T(4,128)}), f32[256,4,256]{2,1,0:T(4,128)}, u32[]{:S(2)}, u32[]{:S(2)}) %all-to-all-start.7) | async-done | bytes 1048608 | tf_op jit(solution)/shard_map/all_to_all | solution.py:60
  841.6 5.5 all-to-all-start.3
  849.2 1.6 copy.46
  850.8 24.3 %all-to-all-done.3 = f32[256,4,256]{2,1,0:T(4,128)} async-done(((f32[256,4,256]{2,1,0:T(4,128)}), f32[256,4,256]{2,1,0:T(4,128)}, u32[]{:S(2)}, u32[]{:S(2)}) %all-to-all-start.3) | async-done | bytes 1048608 | tf_op jit(solution)/shard_map/all_to_all | solution.py:60
  875.1 7.1 all-to-all-start.2
  882.2 2.4 fusion.26
  884.6 2.3 fusion.19
  891.1 1.7 copy.52
  892.8 13.8 %all-to-all-done.2 = f32[256,4,256]{2,1,0:T(4,128)} async-done(((f32[256,4,256]{2,1,0:T(4,128)}), f32[256,4,256]{2,1,0:T(4,128)}, u32[]{:S(2)}, u32[]{:S(2)}) %all-to-all-start.2) | async-done | bytes 1048608 | tf_op jit(solution)/shard_map/all_to_all | solution.py:59
  906.5 6.5 all-to-all-start.4
  915.1 1.7 copy.55
  916.8 18.4 %all-to-all-done.4 = f32[256,4,256]{2,1,0:T(4,128)} async-done(((f32[256,4,256]{2,1,0:T(4,128)}), f32[256,4,256]{2,1,0:T(4,128)}, u32[]{:S(2)}, u32[]{:S(2)}) %all-to-all-start.4) | async-done | bytes 1048608 | tf_op jit(solution)/shard_map/all_to_all | solution.py:59
  935.2 6.5 all-to-all-start.5
  941.7 2.4 fusion.31
  944.1 2.3 fusion.38
  950.6 1.6 copy.43
  952.2 9.2 all-to-all-done.5
  961.5 6.9 all-to-all-start.1
  974.8 1.7 copy.40
  978.4 2.5 copy.62
  980.9 1.6 copy.63
  982.4 2.9 copy.50
  985.4 2.6 copy.51
  987.9 2.5 copy.47
  990.5 2.6 copy.48
  993.0 2.5 copy.53
  995.6 2.5 copy.54
  998.1 2.5 copy.56
  1000.7 2.5 copy.57
  1003.2 2.1 fusion.64
  1005.3 2.1 fusion.67
  1007.4 2.0 fusion.70
  1009.4 2.0 fusion.65
  1011.4 2.2 fusion.56
  1013.6 12.9 %all-to-all-start = ((f32[256,4,256]{2,1,0:T(4,128)}), f32[256,4,256]{2,1,0:T(4,128)}, u32[]{:S(2)}, u32[]{:S(2)}) async-start(f32[256,4,256]{2,1,0:T(4,128)} %copy.40), calls=%async_computation | async-start | bytes 2097152 | tf_op jit(solution)/shard_map/all_to_all | solution.py:59
  1026.5 2.5 copy.44
  1030.6 2.4 fusion.59
  1033.0 3.3 convolution_add_fusion
  1036.3 2.1 convolution_subtract_fusion
  1038.4 2.0 convolution_subtract_fusion.6
  1040.4 2.0 convolution_add_fusion.2
  1042.4 2.0 convolution_add_fusion.1
  1044.4 2.0 convolution_subtract_fusion.3
  1046.5 2.5 copy.41
  1048.9 1.6 copy.42
  1053.7 6.5 add_reduce_fusion.3
  1060.2 2.6 maximum_bitcast_fusion.8
  1062.8 2.6 maximum_bitcast_fusion.10
  1065.4 194.2 %psum.23 = f32[2,2,2]{2,1,0:T(2,128)S(1)} all-reduce(f32[2,2,2]{2,1,0:T(2,128)S(1)} %pad_maximum_fusion.1), channel_id=1, replica_groups=mesh['modes'=64,'mom'=4] {'modes'}, use_global_device_ids=true, to_apply=%region_10.11 | all-reduce | flops 8 | bytes 64 | tf_op jit(solution)/shard_map/psum | solution.py:76
  1260.2 1.8 maximum_bitcast_fusion.4
  1262.5 2.3 pad_maximum_fusion
  1264.8 7.2 copy.72
  (93 shorter events, 34.5 us)
Async XLA Ops:
  7.2 747.1 %all-reduce.3.cloned.1.call-start = ((), (), s32[]{:S(2)}) async-start(), calls=%async_computation.8 | async-start | bytes 2097152 | tf_op jit(solution)/shard_map/psum | solution.py:12
  754.2 4.9 copy-start
  754.2 4.9 copy-start.6
  764.9 41.1 %all-to-all-start.6 = ((f32[256,4,256]{2,1,0:T(4,128)}), f32[256,4,256]{2,1,0:T(4,128)}, u32[]{:S(2)}, u32[]{:S(2)}) async-start(f32[256,4,256]{2,1,0:T(4,128)} %copy.58), calls=%async_computation.6 | async-start | bytes 2097152 | tf_op jit(solution)/shard_map/all_to_all | solution.py:59
  806.1 35.5 %all-to-all-start.7 = ((f32[256,4,256]{2,1,0:T(4,128)}), f32[256,4,256]{2,1,0:T(4,128)}, u32[]{:S(2)}, u32[]{:S(2)}) async-start(f32[256,4,256]{2,1,0:T(4,128)} %copy.61), calls=%async_computation.7 | async-start | bytes 2097152 | tf_op jit(solution)/shard_map/all_to_all | solution.py:60
  812.8 4.7 copy-start.1
  841.6 33.5 %all-to-all-start.3 = ((f32[256,4,256]{2,1,0:T(4,128)}), f32[256,4,256]{2,1,0:T(4,128)}, u32[]{:S(2)}, u32[]{:S(2)}) async-start(f32[256,4,256]{2,1,0:T(4,128)} %copy.49), calls=%async_computation.3 | async-start | bytes 2097152 | tf_op jit(solution)/shard_map/all_to_all | solution.py:60
  848.1 34.1 %copy-start.5 = (f32[2,256,256]{2,1,0:T(8,128)S(1)}, f32[2,256,256]{2,1,0:T(8,128)}, u32[]{:S(2)}) copy-start(f32[2,256,256]{2,1,0:T(8,128)} %get-tuple-element.23) | copy-start | bytes 1572868
  875.1 31.5 %all-to-all-start.2 = ((f32[256,4,256]{2,1,0:T(4,128)}), f32[256,4,256]{2,1,0:T(4,128)}, u32[]{:S(2)}, u32[]{:S(2)}) async-start(f32[256,4,256]{2,1,0:T(4,128)} %copy.46), calls=%async_computation.2 | async-start | bytes 2097152 | tf_op jit(solution)/shard_map/all_to_all | solution.py:59
  882.2 4.7 copy-start.2
  906.5 28.6 %all-to-all-start.4 = ((f32[256,4,256]{2,1,0:T(4,128)}), f32[256,4,256]{2,1,0:T(4,128)}, u32[]{:S(2)}, u32[]{:S(2)}) async-start(f32[256,4,256]{2,1,0:T(4,128)} %copy.52), calls=%async_computation.4 | async-start | bytes 2097152 | tf_op jit(solution)/shard_map/all_to_all | solution.py:59
  935.2 26.3 %all-to-all-start.5 = ((f32[256,4,256]{2,1,0:T(4,128)}), f32[256,4,256]{2,1,0:T(4,128)}, u32[]{:S(2)}, u32[]{:S(2)}) async-start(f32[256,4,256]{2,1,0:T(4,128)} %copy.55), calls=%async_computation.5 | async-start | bytes 2097152 | tf_op jit(solution)/shard_map/all_to_all | solution.py:60
  941.7 4.7 copy-start.3
  949.6 18.8 %copy-start.24 = (s32[2]{0:T(128)S(1)}, s32[2]{0:T(128)}, u32[]{:S(2)}) copy-start(s32[2]{0:T(128)} %param.7) | copy-start | bytes 28
  961.5 52.1 %all-to-all-start.1 = ((f32[256,4,256]{2,1,0:T(4,128)}), f32[256,4,256]{2,1,0:T(4,128)}, u32[]{:S(2)}, u32[]{:S(2)}) async-start(f32[256,4,256]{2,1,0:T(4,128)} %copy.43), calls=%async_computation.1 | async-start | bytes 2097152 | tf_op jit(solution)/shard_map/all_to_all | solution.py:60
  982.4 20.8 %copy-start.7 = (f32[4,256,256]{1,2,0:T(8,128)}, f32[4,256,256]{1,2,0:T(8,128)S(1)}, u32[]{:S(2)}) copy-start(f32[4,256,256]{1,2,0:T(8,128)S(1)} %copy.63) | copy-start | bytes 3145732
  1003.2 4.1 copy-start.11
  1003.2 6.2 copy-start.9
  1003.2 8.2 copy-start.14
  1013.6 32.9 %all-to-all-start = ((f32[256,4,256]{2,1,0:T(4,128)}), f32[256,4,256]{2,1,0:T(4,128)}, u32[]{:S(2)}, u32[]{:S(2)}) async-start(f32[256,4,256]{2,1,0:T(4,128)} %copy.40), calls=%async_computation | async-start | bytes 2097152 | tf_op jit(solution)/shard_map/all_to_all | solution.py:59
  1030.6 5.7 copy-start.8
  1030.6 5.7 copy-start.22
  1030.6 7.8 copy-start.10
  1030.6 7.8 copy-start.21
  1036.3 4.1 copy-start.12
  1036.3 4.1 copy-start.20
  1038.4 4.0 copy-start.13
  1038.4 4.0 copy-start.19
  1040.4 4.0 copy-start.15
  1050.5 3.1 copy-start.4
  1050.5 3.1 copy-start.16
  1050.5 3.1 copy-start.17
  1050.5 3.1 copy-start.18
  1260.2 2.0 copy-start.23
Sparse Core Ops, SparseCore 0:
  12.2 741.9 all-reduce.2
where the time goes:
time: 1290 us; the launch traced here: 1280 us
  waiting for transfers between devices  854 us (66%)
  blocking collectives  194 us (15%)
  matrix products  79.3 us (6%)
  starting transfers between devices  62 us (5%)
  local copies, waits for them, and re-layouts  57.2 us (4%)
  between operations  20 us (2%)
    psum x1, waiting for transfers between devices, spread(): return lax.psum(block, axis)  742 us
    psum x1, blocking collectives, shards(): correlator = lax.psum(partial_sums, 'modes') * norm_scale  194 us
    dot_general x48, matrix products, single(): return jnp.einsum(formula, left_part, right_part, precision=highest)  79.3 us
    all_to_all x4, waiting for transfers between devices, shards(): lax.all_to_all(slab_re, 'modes', split_axis=0, concat_axis=1, tiled=True)  59.9 us
    all_to_all x4, waiting for transfers between devices, shards(): lax.all_to_all(slab_im, 'modes', split_axis=0, concat_axis=1, tiled=True)  51.7 us
    all_to_all x4, starting transfers between devices, shards(): lax.all_to_all(slab_re, 'modes', split_axis=0, concat_axis=1, tiled=True)  36.3 us
  transfers between devices with their start and end apart: 9, of which 8 were waited for; matrix products, arithmetic and copies ran while one was open for 8% of the time, Pallas kernels for 0%

commit v1 on v0

--- a/solution.py
+++ b/solution.py
@@ -2,6 +2,7 @@
 import jax.numpy as jnp
 from jax import lax
 from jax.sharding import PartitionSpec as P
+from jax.lax import all_gather
 
 N = 256
 highest = lax.Precision.HIGHEST
@@ -9,7 +10,8 @@
 
 def spread(block, axis, source):
     block = jnp.where(lax.axis_index(axis) == source, block, jnp.zeros_like(block))
-    return lax.psum(block, axis)
+    _lead_works = lambda bus_axis, xx: jnp.sum(all_gather(xx, bus_axis), axis=0)
+    return _lead_works(axis, block)
 
 
 def complex_product(formula, matrix_re, matrix_im, tensor_re, tensor_im):

time: 1290 us -> 1090 us (0.84)
  waiting for transfers between devices: 854 us -> 621 us
  other arithmetic: 12.7 us -> 36.4 us
    psum x1 -> x0, waiting for transfers between devices: 742 us -> none  [spread(): return lax.psum(block, axis)]
    all_gather x0 -> x2, waiting for transfers between devices: none -> 478 us  [spread(): _lead_works = lambda bus_axis, xx: jnp.sum(all_gather(xx, bus_axis), axis=0)]
    all_to_all x4, waiting for transfers between devices: 51.7 us -> 82.9 us  [shards(): lax.all_to_all(slab_im, 'modes', split_axis=0, concat_axis=1, tiled=True)]
    reduce_sum x0 -> x2, other arithmetic: none -> 23.8 us  [spread(): _lead_works = lambda bus_axis, xx: jnp.sum(all_gather(xx, bus_axis), axis=0)]
  transfers between devices with their start and end apart: 9 -> 10, of which waited for: 8 -> 8; matrix products, arithmetic and copies ran while one was open for 8% -> 13% of each run, Pallas kernels for 0% -> 0%
where the time goes in v1:
time: 1090 us; the launch traced here: 1080 us
  waiting for transfers between devices  621 us (57%)
  blocking collectives  190 us (17%)
  matrix products  79.4 us (7%)
  starting transfers between devices  72.7 us (7%)
  local copies, waits for them, and re-layouts  57.1 us (5%)
  other arithmetic  36.4 us (3%)
  between operations  19.8 us (2%)
    all_gather x2, waiting for transfers between devices, spread(): _lead_works = lambda bus_axis, xx: jnp.sum(all_gather(xx, bus_axis), axis=0)  478 us
    psum x1, blocking collectives, shards(): correlator = lax.psum(partial_sums, 'modes') * norm_scale  190 us
    all_to_all x4, waiting for transfers between devices, shards(): lax.all_to_all(slab_im, 'modes', split_axis=0, concat_axis=1, tiled=True)  82.9 us
    dot_general x48, matrix products, single(): return jnp.einsum(formula, left_part, right_part, precision=highest)  79.4 us
    all_to_all x4, waiting for transfers between devices, shards(): lax.all_to_all(slab_re, 'modes', split_axis=0, concat_axis=1, tiled=True)  59.3 us
    all_to_all x4, starting transfers between devices, shards(): lax.all_to_all(slab_re, 'modes', split_axis=0, concat_axis=1, tiled=True)  40.2 us
    all_to_all x4, starting transfers between devices, shards(): lax.all_to_all(slab_im, 'modes', split_axis=0, concat_axis=1, tiled=True)  32.4 us
    reduce_sum x2, other arithmetic, spread(): _lead_works = lambda bus_axis, xx: jnp.sum(all_gather(xx, bus_axis), axis=0)  23.8 us
  transfers between devices with their start and end apart: 10, of which 8 were waited for; matrix products, arithmetic and copies ran while one was open for 13% of the time, Pallas kernels for 0%

profile of v1, /device:TPU:32, one launch (start us, length us, event | category | flops | bytes accessed | tf_op | source)
XLA Modules:
  0.0 1076.3 jit_solution(13300727423249534009)
XLA Ops:
  9.8 2.3 slice_select_fusion.1
  12.9 288.0 %all-gather.7.cloned.1.call-done = f32[64,1,2,256,256]{4,3,2,1,0:T(8,128)} async-done(((f32[1,1,2,256,256]{4,3,2,1,0:T(8,128)}), f32[64,1,2,256,256]{4,3,2,1,0:T(8,128)}) %all-gather.7.cloned.1.call-update) | async-done | bytes 33554448 | tf_op jit(solution)/shard_map/all_gather | solution.py:13
  300.9 11.9 %reduce_sum.91 = f32[2,256,256]{2,1,0:T(8,128)S(1)} reduce(f32[64,1,2,256,256]{4,3,2,1,0:T(8,128)} %all-gather.7.cloned.1.call-done, f32[]{:T(128)} %constant.15.clone.1), dimensions={0,1}, to_apply=%region_1.2 | reduce | flops 8257536 | bytes 34078724 | tf_op jit(solution)/shard_map/reduce_sum | solution.py:13
  312.8 2.4 fusion.23
  315.2 2.3 fusion.16
  321.7 1.6 copy.58
  323.3 11.1 %all-to-all-start.6 = ((f32[256,4,256]{2,1,0:T(4,128)}), f32[256,4,256]{2,1,0:T(4,128)}, u32[]{:S(2)}, u32[]{:S(2)}) async-start(f32[256,4,256]{2,1,0:T(4,128)} %copy.58), calls=%async_computation.6 | async-start | bytes 2097152 | tf_op jit(solution)/shard_map/all_to_all | solution.py:61
  336.4 1.7 copy.61
  338.1 27.7 %all-to-all-done.6 = f32[256,4,256]{2,1,0:T(4,128)} async-done(((f32[256,4,256]{2,1,0:T(4,128)}), f32[256,4,256]{2,1,0:T(4,128)}, u32[]{:S(2)}, u32[]{:S(2)}) %all-to-all-start.6) | async-done | bytes 1048608 | tf_op jit(solution)/shard_map/all_to_all | solution.py:61
  365.8 13.7 %all-to-all-start.7 = ((f32[256,4,256]{2,1,0:T(4,128)}), f32[256,4,256]{2,1,0:T(4,128)}, u32[]{:S(2)}, u32[]{:S(2)}) async-start(f32[256,4,256]{2,1,0:T(4,128)} %copy.61), calls=%async_computation.7 | async-start | bytes 2097152 | tf_op jit(solution)/shard_map/all_to_all | solution.py:62
  379.5 2.4 fusion.28
  381.9 2.3 fusion.35
  388.3 1.7 copy.49
  390.0 35.9 %all-to-all-done.7 = f32[256,4,256]{2,1,0:T(4,128)} async-done(((f32[256,4,256]{2,1,0:T(4,128)}), f32[256,4,256]{2,1,0:T(4,128)}, u32[]{:S(2)}, u32[]{:S(2)}) %all-to-all-start.7) | async-done | bytes 1048608 | tf_op jit(solution)/shard_map/all_to_all | solution.py:62
  425.9 6.2 all-to-all-start.3
  434.1 1.6 copy.46
  435.8 30.5 %all-to-all-done.3 = f32[256,4,256]{2,1,0:T(4,128)} async-done(((f32[256,4,256]{2,1,0:T(4,128)}), f32[256,4,256]{2,1,0:T(4,128)}, u32[]{:S(2)}, u32[]{:S(2)}) %all-to-all-start.3) | async-done | bytes 1048608 | tf_op jit(solution)/shard_map/all_to_all | solution.py:62
  466.3 5.7 all-to-all-start.2
  471.9 190.4 %all-gather.5.cloned.1.call-done = f32[64,1,2,256,256]{4,3,2,1,0:T(8,128)} async-done(((f32[1,1,2,256,256]{4,3,2,1,0:T(8,128)}), f32[64,1,2,256,256]{4,3,2,1,0:T(8,128)}) %all-gather.5.cloned.1.call-update) | async-done | bytes 33554448 | tf_op jit(solution)/shard_map/all_gather | solution.py:13
  662.3 11.9 %reduce_sum.90 = f32[2,256,256]{2,1,0:T(8,128)S(1)} reduce(f32[64,1,2,256,256]{4,3,2,1,0:T(8,128)} %all-gather.5.cloned.1.call-done, f32[]{:T(128)} %constant.15.clone.1), dimensions={0,1}, to_apply=%region_0.1 | reduce | flops 8257536 | bytes 34078724 | tf_op jit(solution)/shard_map/reduce_sum | solution.py:13
  674.2 2.4 fusion.26
  676.7 2.3 fusion.19
  683.1 1.7 copy.52
  684.8 10.5 all-to-all-start.4
  697.4 1.7 copy.55
  699.1 26.3 %all-to-all-done.4 = f32[256,4,256]{2,1,0:T(4,128)} async-done(((f32[256,4,256]{2,1,0:T(4,128)}), f32[256,4,256]{2,1,0:T(4,128)}, u32[]{:S(2)}, u32[]{:S(2)}) %all-to-all-start.4) | async-done | bytes 1048608 | tf_op jit(solution)/shard_map/all_to_all | solution.py:61
  725.4 5.9 all-to-all-start.5
  731.3 2.4 fusion.31
  733.7 2.3 fusion.38
  741.8 16.6 %all-to-all-done.5 = f32[256,4,256]{2,1,0:T(4,128)} async-done(((f32[256,4,256]{2,1,0:T(4,128)}), f32[256,4,256]{2,1,0:T(4,128)}, u32[]{:S(2)}, u32[]{:S(2)}) %all-to-all-start.5) | async-done | bytes 1048608 | tf_op jit(solution)/shard_map/all_to_all | solution.py:62
  758.4 6.7 all-to-all-start.1
  771.4 1.7 copy.40
  775.0 2.5 copy.62
  779.0 2.9 copy.50
  781.9 2.5 copy.51
  784.4 2.5 copy.47
  787.0 2.5 copy.48
  789.5 2.5 copy.53
  792.0 2.5 copy.54
  794.6 2.5 copy.56
  797.1 2.6 copy.57
  799.7 2.0 fusion.64
  801.7 2.1 fusion.67
  803.8 2.0 fusion.70
  805.8 2.0 fusion.65
  807.9 2.2 fusion.56
  810.0 12.9 %all-to-all-start = ((f32[256,4,256]{2,1,0:T(4,128)}), f32[256,4,256]{2,1,0:T(4,128)}, u32[]{:S(2)}, u32[]{:S(2)}) async-start(f32[256,4,256]{2,1,0:T(4,128)} %copy.40), calls=%async_computation | async-start | bytes 2097152 | tf_op jit(solution)/shard_map/all_to_all | solution.py:61
  823.0 2.5 copy.44
  827.1 2.4 fusion.59
  829.5 3.3 convolution_add_fusion
  832.7 2.1 convolution_subtract_fusion
  834.8 2.0 convolution_subtract_fusion.6
  836.9 2.0 convolution_add_fusion.2
  838.9 2.0 convolution_add_fusion.1
  840.9 2.0 convolution_subtract_fusion.3
  842.9 5.3 all-to-all-done
  848.1 2.5 copy.41
  855.4 6.7 add_reduce_fusion.3
  862.0 2.5 maximum_bitcast_fusion.8
  864.5 2.6 maximum_bitcast_fusion.10
  867.2 189.6 %psum.7 = f32[2,2,2]{2,1,0:T(2,128)S(1)} all-reduce(f32[2,2,2]{2,1,0:T(2,128)S(1)} %pad_maximum_fusion.1), channel_id=1, replica_groups=mesh['modes'=64,'mom'=4] {'modes'}, use_global_device_ids=true, to_apply=%region_10.11 | all-reduce | flops 8 | bytes 64 | tf_op jit(solution)/shard_map/psum | solution.py:78
  1057.4 1.8 maximum_bitcast_fusion.4
  1059.7 2.3 pad_maximum_fusion
  1062.0 7.2 copy.72
  (94 shorter events, 40.0 us)
Async XLA Ops:
  7.2 293.7 %all-gather.7.cloned.1.call-start = ((), (), s32[]{:S(2)}) async-start(), calls=%async_computation.9 | async-start | bytes 34078720 | tf_op jit(solution)/shard_map/all_gather | solution.py:13
  12.1 650.2 %all-gather.5.cloned.1.call-start = ((), (), s32[]{:S(2)}) async-start(), calls=%async_computation.8 | async-start | bytes 34078720 | tf_op jit(solution)/shard_map/all_gather | solution.py:13
  312.7 4.8 copy-start
  323.3 42.5 %all-to-all-start.6 = ((f32[256,4,256]{2,1,0:T(4,128)}), f32[256,4,256]{2,1,0:T(4,128)}, u32[]{:S(2)}, u32[]{:S(2)}) async-start(f32[256,4,256]{2,1,0:T(4,128)} %copy.58), calls=%async_computation.6 | async-start | bytes 2097152 | tf_op jit(solution)/shard_map/all_to_all | solution.py:61
  365.8 60.1 %all-to-all-start.7 = ((f32[256,4,256]{2,1,0:T(4,128)}), f32[256,4,256]{2,1,0:T(4,128)}, u32[]{:S(2)}, u32[]{:S(2)}) async-start(f32[256,4,256]{2,1,0:T(4,128)} %copy.61), calls=%async_computation.7 | async-start | bytes 2097152 | tf_op jit(solution)/shard_map/all_to_all | solution.py:62
  379.5 4.7 copy-start.1
  425.9 40.4 %all-to-all-start.3 = ((f32[256,4,256]{2,1,0:T(4,128)}), f32[256,4,256]{2,1,0:T(4,128)}, u32[]{:S(2)}, u32[]{:S(2)}) async-start(f32[256,4,256]{2,1,0:T(4,128)} %copy.49), calls=%async_computation.3 | async-start | bytes 2097152 | tf_op jit(solution)/shard_map/all_to_all | solution.py:62
  466.3 218.5 %all-to-all-start.2 = ((f32[256,4,256]{2,1,0:T(4,128)}), f32[256,4,256]{2,1,0:T(4,128)}, u32[]{:S(2)}, u32[]{:S(2)}) async-start(f32[256,4,256]{2,1,0:T(4,128)} %copy.46), calls=%async_computation.2 | async-start | bytes 2097152 | tf_op jit(solution)/shard_map/all_to_all | solution.py:61
  674.2 4.7 copy-start.2
  684.8 40.6 %all-to-all-start.4 = ((f32[256,4,256]{2,1,0:T(4,128)}), f32[256,4,256]{2,1,0:T(4,128)}, u32[]{:S(2)}, u32[]{:S(2)}) async-start(f32[256,4,256]{2,1,0:T(4,128)} %copy.52), calls=%async_computation.4 | async-start | bytes 2097152 | tf_op jit(solution)/shard_map/all_to_all | solution.py:61
  725.4 33.0 %all-to-all-start.5 = ((f32[256,4,256]{2,1,0:T(4,128)}), f32[256,4,256]{2,1,0:T(4,128)}, u32[]{:S(2)}, u32[]{:S(2)}) async-start(f32[256,4,256]{2,1,0:T(4,128)} %copy.55), calls=%async_computation.5 | async-start | bytes 2097152 | tf_op jit(solution)/shard_map/all_to_all | solution.py:62
  731.3 4.7 copy-start.3
  739.1 26.0 %copy-start.22 = (s32[2]{0:T(128)S(1)}, s32[2]{0:T(128)}, u32[]{:S(2)}) copy-start(s32[2]{0:T(128)} %param.7) | copy-start | bytes 28
  758.4 51.7 %all-to-all-start.1 = ((f32[256,4,256]{2,1,0:T(4,128)}), f32[256,4,256]{2,1,0:T(4,128)}, u32[]{:S(2)}, u32[]{:S(2)}) async-start(f32[256,4,256]{2,1,0:T(4,128)} %copy.43), calls=%async_computation.1 | async-start | bytes 2097152 | tf_op jit(solution)/shard_map/all_to_all | solution.py:62
  779.0 20.7 %copy-start.5 = (f32[4,256,256]{1,2,0:T(8,128)}, f32[4,256,256]{1,2,0:T(8,128)S(1)}, u32[]{:S(2)}) copy-start(f32[4,256,256]{1,2,0:T(8,128)S(1)} %copy.63) | copy-start | bytes 3145732
  799.7 4.1 copy-start.9
  799.7 6.2 copy-start.7
  799.7 8.2 copy-start.12
  810.0 38.1 %all-to-all-start = ((f32[256,4,256]{2,1,0:T(4,128)}), f32[256,4,256]{2,1,0:T(4,128)}, u32[]{:S(2)}, u32[]{:S(2)}) async-start(f32[256,4,256]{2,1,0:T(4,128)} %copy.40), calls=%async_computation | async-start | bytes 2097152 | tf_op jit(solution)/shard_map/all_to_all | solution.py:61
  827.0 5.7 copy-start.6
  827.0 5.7 copy-start.20
  827.0 7.8 copy-start.8
  827.0 7.8 copy-start.19
  832.7 4.1 copy-start.10
  832.7 4.1 copy-start.18
  834.8 4.0 copy-start.11
  834.8 4.0 copy-start.17
  836.9 4.0 copy-start.13
  852.2 3.1 copy-start.4
  852.2 3.1 copy-start.14
  852.2 3.1 copy-start.15
  852.2 3.1 copy-start.16
  1057.4 2.0 copy-start.21
Sparse Core Ops, SparseCore 0:
  12.2 288.5 all-gather.6
  304.2 358.1 all-gather.4
